TPU v7x, 32 devices: a whole 2x2x4 slice. The times are simulated.
32 devices in a mesh: tower: 8 (over z, x), plate: 4 (over y, core).
Axes of the slice: x: 2, y: 2, z: 4, core: 2. Of those that a mesh axis runs over, the one named last changes fastest.
Arguments:
- features: bfloat16 [8, 1024, 128], P('tower', 'plate'), may hold values from -6 to 6
- adjoint: bfloat16 [8, 1024, 128], P('tower', 'plate'), may hold values from -6 to 6
- positions: bfloat16 [3, 8, 1024], P(None, 'tower', 'plate'), may hold values from 0 to 1
- w_rbf: bfloat16 [16, 128], replicated, may hold values from -1.5 to 1.5
- b_rbf: float32 [128], replicated, may hold values from -1 to 1
- w_filter: bfloat16 [128, 128], replicated, may hold values from -0.5 to 0.5
- b_filter: float32 [128], replicated, may hold values from -1 to 1
- atom_counts: int32 [8, 4], P('tower', 'plate'), may hold values from 128 to 256, as said below
- tile_counts: int32 [8, 4], P('tower', 'plate'), may hold values from 1 to 56, as said below
- tower_tiles: int32 [8, 4, 56], P('tower', 'plate'), may hold values from 0 to 23
- plate_tiles: int32 [8, 4, 56], P('tower', 'plate'), may hold values from 0 to 31
- image_shifts: int32 [8, 4, 56], P('tower', 'plate'), may hold values from 0 to 8
Outputs:
- grad_features: float32 [8, 1024, 128], P('tower', 'plate')
- grad_positions: float32 [3, 8, 1024], P(None, 'tower', 'plate')
- grad_w_rbf: float32 [16, 128], replicated
- grad_b_rbf: float32 [128], replicated
- grad_w_filter: float32 [128, 128], replicated
- grad_b_filter: float32 [128], replicated
Inputs may be any that keep to these rules, and one draw needn't show every extreme that they name: `atom_counts`: 256 in at least one brick. `tile_counts`: 56 in at least one brick; entries past the count are unused. `tower_tiles`: tiles below 8 lie in the brick below, the next 8 in the brick itself, the rest in the brick above. `plate_tiles`: tile v lies in brick v // 8 of the same plate. `image_shifts`: shift c moves the receiver by c // 3 - 1 along x and c % 3 - 1 along y.
All inputs are finite; a program needn't handle non-finite values.
Results may differ from a plain program's by a relative error of at most 0.005.
Values may be sent and summed in bfloat16 or wider, within the bound.
No kernel may reach another device: no remote copies, remote signals or barrier semaphores. Data moves between devices by JAX's collectives and lax.ppermute only.
A program may use at most 64 MiB of HBM per device.

v0:
```python
import math
import jax
import jax.numpy as jnp
from jax import lax
from jax.sharding import PartitionSpec as P

TILE = 32
box_side = 1.0
brick_height = 1.0
cutoff_radius = 3.0
soften = 0.01
sharpness = 10.0
log_two = math.log(2.0)


def shifted(block, axis, distance):
    devices = range(lax.axis_size(axis))
    route = [((i - distance) % len(devices), i) for i in devices]
    return lax.ppermute(block, axis, route)


def shift_vector(shift_code, tower_tile, per_brick):
    step_z = tower_tile // per_brick - 1
    return jnp.stack(
        [
            (shift_code // 3 - 1).astype(jnp.float32) * box_side,
            (shift_code % 3 - 1).astype(jnp.float32) * box_side,
            step_z.astype(jnp.float32) * brick_height,
        ]
    )


def pair_tile(adj_rows, recv_pos, feat_rows, send_pos, shift_vec, w_rbf, b_rbf, w_filter, b_filter):
    size_recv = adj_rows.shape[0]
    size_send = feat_rows.shape[0]
    feat_width = adj_rows.shape[1]
    displace = recv_pos[:, :, None] + shift_vec[:, None, None] - send_pos[:, None, :]
    distance = jnp.sqrt(jnp.sum(displace * displace, axis=0) + soften).reshape(-1)
    nbasis = w_rbf.shape[0]
    centres = jnp.arange(nbasis, dtype=jnp.float32) * (cutoff_radius / (nbasis - 1))
    offsets = distance[None, :] - centres[:, None]
    basis = jnp.exp(-sharpness * offsets * offsets)
    basis_b = basis.astype(jnp.bfloat16)
    preact = (
        lax.dot_general(
            basis_b, w_rbf, (((0,), (0,)), ((), ())), preferred_element_type=jnp.float32
        )
        + b_rbf
    )
    softed = (jax.nn.softplus(preact) - log_two).astype(jnp.bfloat16)
    filter_raw = jnp.dot(softed, w_filter, preferred_element_type=jnp.float32) + b_filter
    inside = distance < cutoff_radius
    phase_arg = math.pi / cutoff_radius * distance
    envelope = jnp.where(inside, 0.5 * (jnp.cos(phase_arg) + 1.0), 0.0)
    slope = jnp.where(inside, -0.5 * (math.pi / cutoff_radius) * jnp.sin(phase_arg), 0.0)
    adj_wide = adj_rows.astype(jnp.float32)
    feat_wide = feat_rows.astype(jnp.float32)
    filtered = (filter_raw * envelope[:, None]).reshape(size_recv, size_send, feat_width)
    grad_rows = jnp.einsum("if,ijf->jf", adj_wide, filtered)
    adjoint_pair = (adj_wide[:, None, :] * feat_wide[None, :, :]).reshape(
        size_recv * size_send, feat_width
    )
    d_raw = adjoint_pair * envelope[:, None]
    d_raw_b = d_raw.astype(jnp.bfloat16)
    grad_bf = jnp.sum(d_raw, axis=0)
    grad_wf = lax.dot_general(
        softed, d_raw_b, (((0,), (0,)), ((), ())), preferred_element_type=jnp.float32
    )
    d_soft = lax.dot_general(
        d_raw_b, w_filter, (((1,), (1,)), ((), ())), preferred_element_type=jnp.float32
    )
    d_pre = d_soft * jax.nn.sigmoid(preact)
    d_pre_b = d_pre.astype(jnp.bfloat16)
    grad_br = jnp.sum(d_pre, axis=0)
    grad_wr = lax.dot_general(
        basis_b, d_pre_b, (((1,), (0,)), ((), ())), preferred_element_type=jnp.float32
    )
    d_basis = lax.dot_general(
        w_rbf, d_pre_b, (((1,), (1,)), ((), ())), preferred_element_type=jnp.float32
    )
    d_dist = jnp.sum(d_basis * basis * (-2.0 * sharpness) * offsets, axis=0)
    d_dist = d_dist + jnp.sum(adjoint_pair * filter_raw, axis=1) * slope
    radial = (d_dist / distance).reshape(size_recv, size_send)
    pull = displace * radial[None]
    return (
        grad_rows,
        jnp.sum(pull, axis=2),
        -jnp.sum(pull, axis=1),
        (grad_wr, grad_br, grad_wf, grad_bf),
    )


def add_into(array, piece, starts):
    current = lax.dynamic_slice(array, starts, piece.shape)
    return lax.dynamic_update_slice(array, current + piece, starts)


def add_weights(left, right):
    return jax.tree.map(lambda first_term, second_term: first_term + second_term, left, right)


def local(
    features,
    adjoint,
    positions,
    w_rbf,
    b_rbf,
    w_filter,
    b_filter,
    atom_counts,
    tile_counts,
    tower_tiles,
    plate_tiles,
    image_shifts,
):
    brick_atoms = features.shape[1]
    feat_width = features.shape[2]
    tile_size = TILE
    per_brick = brick_atoms // tile_size
    plate_count = lax.axis_size("plate")
    zero_i = jnp.int32(0)
    live_mask = jnp.arange(brick_atoms, dtype=jnp.int32) < atom_counts[0, 0]
    zero_b = jnp.zeros((), jnp.bfloat16)
    own_feat = jnp.where(live_mask[:, None], features[0], zero_b)
    own_adj = jnp.where(live_mask[:, None], adjoint[0], zero_b)
    own_pos = positions[:, 0, :]
    from_below = shifted((own_adj, own_pos), "tower", 1)
    from_above = shifted((own_adj, own_pos), "tower", -1)
    tower_adj = jnp.concatenate([from_below[0], own_adj, from_above[0]], axis=0)
    tower_pos_b = jnp.concatenate([from_below[1], own_pos, from_above[1]], axis=1)
    tower_pos = tower_pos_b.astype(jnp.float32)
    weight_zero = (
        jnp.zeros(w_rbf.shape, jnp.float32),
        jnp.zeros(b_rbf.shape, jnp.float32),
        jnp.zeros(w_filter.shape, jnp.float32),
        jnp.zeros(b_filter.shape, jnp.float32),
    )
    plate_feat, plate_pos_b = (
        lax.all_gather(own_feat, "plate", axis=0, tiled=True),
        lax.all_gather(own_pos, "plate", axis=1, tiled=True),
    )
    plate_pos = plate_pos_b.astype(jnp.float32)

    def visit_listed(entry, totals):
        acc_dh, acc_gp, acc_tower, acc_weights = totals
        tower_tile = tower_tiles[0, 0, entry]
        plate_tile = plate_tiles[0, 0, entry]
        recv_start = tower_tile * tile_size
        send_start = plate_tile * tile_size
        adj_rows = lax.dynamic_slice_in_dim(tower_adj, recv_start, tile_size, 0)
        recv_pos = lax.dynamic_slice_in_dim(tower_pos, recv_start, tile_size, 1)
        feat_rows = lax.dynamic_slice_in_dim(plate_feat, send_start, tile_size, 0)
        send_pos = lax.dynamic_slice_in_dim(plate_pos, send_start, tile_size, 1)
        shift_vec = shift_vector(image_shifts[0, 0, entry], tower_tile, per_brick)
        grad_rows, grad_recv, grad_send, grad_weights = pair_tile(
            adj_rows, recv_pos, feat_rows, send_pos, shift_vec, w_rbf, b_rbf, w_filter, b_filter
        )
        brick_index = plate_tile // per_brick
        local_start = plate_tile % per_brick * tile_size
        acc_dh = add_into(acc_dh, grad_rows[None], (brick_index, local_start, zero_i))
        acc_gp = add_into(acc_gp, grad_send[None], (brick_index, zero_i, local_start))
        acc_tower = add_into(acc_tower, grad_recv, (zero_i, recv_start))
        return (acc_dh, acc_gp, acc_tower, add_weights(acc_weights, grad_weights))

    initial = (
        jnp.zeros((plate_count, brick_atoms, feat_width), jnp.float32),
        jnp.zeros((plate_count, 3, brick_atoms), jnp.float32),
        jnp.zeros((3, 3 * brick_atoms), jnp.float32),
        weight_zero,
    )
    acc_dh, acc_gp, tower_grad, acc_weights = lax.fori_loop(
        0, tile_counts[0, 0], visit_listed, initial
    )
    home_dh, home_gp = (
        lax.psum_scatter(acc_dh, "plate", scatter_dimension=0, tiled=True),
        lax.psum_scatter(acc_gp, "plate", scatter_dimension=0, tiled=True),
    )
    plate_dh = home_dh[0]
    plate_gp = home_gp[0]
    back_down = shifted(tower_grad[:, :brick_atoms], "tower", -1)
    back_up = shifted(tower_grad[:, 2 * brick_atoms :], "tower", 1)
    total_pos = plate_gp + tower_grad[:, brick_atoms : 2 * brick_atoms] + back_down + back_up
    tile_total = tile_counts[0, 0].astype(jnp.float32)
    summed = lax.psum(
        (acc_weights[0], acc_weights[1], acc_weights[2], acc_weights[3], tile_total),
        ("tower", "plate"),
    )
    scale = lax.rsqrt(summed[4] * (tile_size * tile_size))
    grad_features = jnp.where(live_mask[:, None], plate_dh, 0.0)[None]
    grad_positions = total_pos.reshape(3, 1, brick_atoms)
    return (
        grad_features,
        grad_positions,
        summed[0] * scale,
        summed[1] * scale,
        summed[2] * scale,
        summed[3] * scale,
    )


def solution(mesh):
    in_specs = (
        P("tower", "plate", None),
        P("tower", "plate", None),
        P(None, "tower", "plate"),
        P(),
        P(),
        P(),
        P(),
        P("tower", "plate"),
        P("tower", "plate"),
        P("tower", "plate", None),
        P("tower", "plate", None),
        P("tower", "plate", None),
    )
    out_specs = (P("tower", "plate", None), P(None, "tower", "plate"), P(), P(), P(), P())
    return jax.shard_map(local, mesh=mesh, in_specs=in_specs, out_specs=out_specs, check_vma=False)
```

profile of v0, /device:TPU:1, one launch (start us, length us, event | category | flops | bytes accessed | tf_op | source)
XLA Modules:
  0.0 1107.9 jit_solution(14880807231153509916)
XLA Ops:
  8.7 1.0 bitcast_select_fusion
  9.7 2.1 collective-permute-start.2
  11.8 3.1 collective-permute-start.3
  14.9 4.2 collective-permute-start.1
  19.0 6.5 all-gather
  25.6 5.9 all_gather.7
  31.7 0.6 copy-done.6
  32.4 304.2 %while.25 = (s32[]{:T(128)}, f32[4,256,128]{2,1,0:T(8,128)S(1)}, f32[4,3,256]{2,1,0:T(4,128)S(1)}, f32[3,768]{1,0:T(4,128)S(1)}, f32[16,128]{1,0:T(8,128)S(1)}, ...) while((s32[]{:T(128)}, f32[4,256,128]{2,1,0:T(8,128)S(1)}, ...), condition=%wide.region_8.9_spmd, body=%wide.region_0.8_spmd.sunk | while | flops 118017312 | bytes 6281055 | solution.py:171
  36.2 0.6 fusion.71
  41.5 0.6 constant_dynamic-slice_fusion.10
  43.7 0.6 fusion.73
  53.2 0.6 fusion.71
  58.4 0.6 constant_dynamic-slice_fusion.10
  60.6 0.6 fusion.73
  70.0 0.6 fusion.71
  75.2 0.6 constant_dynamic-slice_fusion.10
  77.4 0.6 fusion.73
  86.9 0.6 fusion.71
  92.1 0.6 constant_dynamic-slice_fusion.10
  94.4 0.6 fusion.73
  103.8 0.6 fusion.71
  109.1 0.6 constant_dynamic-slice_fusion.10
  111.3 0.6 fusion.73
  120.6 0.6 fusion.71
  125.9 0.6 constant_dynamic-slice_fusion.10
  128.1 0.6 fusion.73
  137.6 0.6 fusion.71
  145.0 0.6 fusion.73
  154.5 0.6 fusion.71
  161.9 0.6 fusion.73
  171.3 0.6 fusion.71
  178.7 0.6 fusion.73
  188.2 0.6 fusion.71
  195.7 0.6 fusion.73
  205.1 0.6 fusion.71
  210.3 0.6 constant_dynamic-slice_fusion.10
  212.6 0.6 fusion.73
  222.0 0.6 fusion.71
  227.2 0.6 constant_dynamic-slice_fusion.10
  229.5 0.6 fusion.73
  238.8 0.6 fusion.71
  246.3 0.6 fusion.73
  255.6 0.6 fusion.71
  263.0 0.6 fusion.73
  272.4 0.6 fusion.71
  277.6 0.6 constant_dynamic-slice_fusion.10
  279.8 0.6 fusion.73
  289.3 0.6 fusion.71
  296.8 0.6 fusion.73
  306.1 0.6 fusion.71
  313.6 0.6 fusion.73
  322.9 0.6 fusion.71
  328.1 0.6 constant_dynamic-slice_fusion.10
  330.4 0.6 fusion.73
  336.7 0.6 copy-done.1
  338.0 0.6 copy-done.10
  339.2 678.0 %all-reduce.1 = (f32[16,128]{1,0:T(8,128)S(1)}, f32[]{:T(128)}, f32[128]{0:T(128)S(1)}, f32[128]{0:T(128)S(1)}) all-reduce(f32[16,128]{1,0:T(8,128)S(1)} %get-tuple-element.335, f32[]{:T(128)S(6)} %convert_element_type.74, f32[128]{0:T(128)S(1)} %get-tuple-element.336, ...), channel_id=1, replica_groups=mesh['tower'=8,'plate'=4] {'tower','plate'}, use_global_device_ids=true, to_apply=%region_11.12 | all-reduce | flops 2305 | bytes 18440 | tf_op jit(solution)/shard_map/psum | solution.py:184
  1018.0 1.9 collective-permute-start.4
  1020.5 0.6 broadcast_multiply_fusion.3
  1021.1 10.9 all-reduce
  1032.0 0.7 fusion.28
  1033.3 64.1 %all-reduce.4.cloned.1.call-done = f32[128,128]{1,0:T(8,128)} async-done(((f32[128,128]{1,0:T(8,128)}), f32[128,128]{1,0:T(8,128)}) %all-reduce.4.cloned.1.call-update) | async-done | bytes 65552 | tf_op jit(solution)/shard_map/psum | solution.py:184
  1097.3 1.5 broadcast_multiply_fusion.2
  1098.8 1.7 broadcast_select_fusion
  (541 shorter events, 76.6 us)
Async XLA Ops:
  8.0 1089.3 %all-reduce.4.cloned.1.call-start = ((), (), s32[]{:S(2)}) async-start(), calls=%async_computation.2 | async-start | bytes 131072 | tf_op jit(solution)/shard_map/psum | solution.py:184
  9.7 5.2 copy-start.5
  9.7 21.8 %collective-permute-start.2 = (bf16[256,128]{1,0:T(8,128)(2,1)S(1)}, bf16[256,128]{1,0:T(8,128)(2,1)S(1)}, u32[]{:S(2)}, u32[]{:S(2)}) collective-permute-start(bf16[256,128]{1,0:T(8,128)(2,1)S(1)} %get-tuple-element.416), channel_id=1, source_target_pairs={{28,0},{0,4},{4,8},{8,12},{12,16},{16,20},{20,24},{24,28},{29,1},{... | collective-permute-start | bytes 196616 | tf_op jit(solution)/shard_map/ppermute | solution.py:19
  11.8 19.7 %collective-permute-start.3 = (bf16[256,128]{1,0:T(8,128)(2,1)S(1)}, bf16[256,128]{1,0:T(8,128)(2,1)S(1)}, u32[]{:S(2)}, u32[]{:S(2)}) collective-permute-start(bf16[256,128]{1,0:T(8,128)(2,1)S(1)} %get-tuple-element.416), channel_id=1, source_target_pairs={{4,0},{8,4},{12,8},{16,12},{20,16},{24,20},{28,24},{0,28},{5,1},{9... | collective-permute-start | bytes 196616 | tf_op jit(solution)/shard_map/ppermute | solution.py:19
  14.9 16.6 %collective-permute-start = (bf16[3,256]{1,0:T(4,128)(2,1)S(1)}, bf16[3,256]{1,0:T(4,128)(2,1)S(1)}, u32[]{:S(2)}, u32[]{:S(2)}) collective-permute-start(bf16[3,256]{1,0:T(4,128)(2,1)S(1)} %bitcast.114), channel_id=1, source_target_pairs={{28,0},{0,4},{4,8},{8,12},{12,16},{16,20},{20,24},{24,28},{29,1},{... | collective-permute-start | bytes 4616 | tf_op jit(solution)/shard_map/ppermute | solution.py:19
  14.9 16.6 %collective-permute-start.1 = (bf16[3,256]{1,0:T(4,128)(2,1)S(1)}, bf16[3,256]{1,0:T(4,128)(2,1)S(1)}, u32[]{:S(2)}, u32[]{:S(2)}) collective-permute-start(bf16[3,256]{1,0:T(4,128)(2,1)S(1)} %bitcast.115), channel_id=1, source_target_pairs={{4,0},{8,4},{12,8},{16,12},{20,16},{24,20},{28,24},{0,28},{5,1},{9... | collective-permute-start | bytes 4616 | tf_op jit(solution)/shard_map/ppermute | solution.py:19
  31.6 0.8 copy-start.6
  31.6 0.7 copy-start.8
  31.6 0.7 copy-start.9
  31.6 0.7 copy-start.2
  31.7 0.7 copy-start.3
  31.7 0.7 copy-start.4
  31.7 0.7 copy-start.7
  336.6 0.6 copy-start.1
  336.6 681.3 %copy-start = (f32[4,256,128]{2,1,0:T(8,128)}, f32[4,256,128]{2,1,0:T(8,128)S(1)}, u32[]{:S(2)}) copy-start(f32[4,256,128]{2,1,0:T(8,128)S(1)} %get-tuple-element.332) | copy-start | bytes 1572868
  337.3 761.5 %reduce-scatter.2.cloned.1.call-start = ((), (), s32[]{:S(2)}) async-start(), calls=%async_computation.1 | async-start | bytes 655360 | tf_op jit(solution)/shard_map/reduce_scatter | solution.py:175
  338.0 0.7 copy-start.10
  1018.0 14.0 %collective-permute-start.4 = (f32[3,256]{1,0:T(4,128)S(1)}, f32[3,256]{1,0:T(4,128)S(1)}, u32[]{:S(2)}, u32[]{:S(2)}) collective-permute-start(f32[3,256]{1,0:T(4,128)S(1)} %get-tuple-element.413), channel_id=1, source_target_pairs={{4,0},{8,4},{12,8},{16,12},{20,16},{24,20},{28,24},{0,28},{5,1},{9... | collective-permute-start | bytes 9224 | tf_op jit(solution)/shard_map/ppermute | solution.py:19
  1019.9 12.1 %collective-permute-start.5 = (f32[3,256]{1,0:T(4,128)S(1)}, f32[3,256]{1,0:T(4,128)S(1)}, u32[]{:S(2)}, u32[]{:S(2)}) collective-permute-start(f32[3,256]{1,0:T(4,128)S(1)} %get-tuple-element.414), channel_id=1, source_target_pairs={{28,0},{0,4},{4,8},{8,12},{12,16},{16,20},{20,24},{24,28},{29,1},{... | collective-permute-start | bytes 9224 | tf_op jit(solution)/shard_map/ppermute | solution.py:19
Sparse Core Ops, SparseCore 0:
  337.4 759.8 all-reduce.3
Sparse Core Ops, SparseCore 1:
  1018.1 22.2 reduce-scatter.1
where the time goes:
time: 1120 us; the launch traced here: 1110 us
  blocking collectives  701 us (63%)
  loops' own time  202 us (18%)
  waiting for transfers between devices  64.1 us (6%)
  matrix products  39.7 us (4%)
  other arithmetic  37 us (3%)
  local copies, waits for them, and re-layouts  34.4 us (3%)
  between operations  17.7 us (2%)
  starting transfers between devices  11.4 us (1%)
    psum x1, blocking collectives, local(): lax.psum((acc_weights[0], acc_weights[1], acc_weights[2], acc_weights[3],...  678 us
    another operation x1, loops' own time, local(): lax.fori_loop(0, tile_counts[0, 0], visit_listed, initial)  202 us
    psum x1, waiting for transfers between devices, local(): lax.psum((acc_weights[0], acc_weights[1], acc_weights[2], acc_weights[3],...  64.1 us
  transfers between devices with their start and end apart: 8, of which 1 were waited for; matrix products, arithmetic and copies ran while one was open for 0% of the time, Pallas kernels for 0%

commit v1 on v0

--- a/solution.py
+++ b/solution.py
@@ -181,10 +181,10 @@
     back_up = shifted(tower_grad[:, 2 * brick_atoms :], "tower", 1)
     total_pos = plate_gp + tower_grad[:, brick_atoms : 2 * brick_atoms] + back_down + back_up
     tile_total = tile_counts[0, 0].astype(jnp.float32)
-    summed = lax.psum(
-        (acc_weights[0], acc_weights[1], acc_weights[2], acc_weights[3], tile_total),
-        ("tower", "plate"),
-    )
+    inner = lax.psum(
+        (acc_weights[0], acc_weights[1], acc_weights[2], acc_weights[3], tile_total), "plate"
+    )
+    summed = lax.psum(inner, "tower")
     scale = lax.rsqrt(summed[4] * (tile_size * tile_size))
     grad_features = jnp.where(live_mask[:, None], plate_dh, 0.0)[None]
     grad_positions = total_pos.reshape(3, 1, brick_atoms)

time: 1120 us -> 1120 us (level)
  waiting for transfers between devices: 64.1 us -> 728 us
  blocking collectives: 701 us -> 43.3 us
    psum x1, blocking collectives: 678 us -> 18.4 us  [local(): summed = lax.psum(inner, 'tower')]
    psum x1, waiting for transfers between devices: 64.1 us -> 669 us  [local(): lax.psum((acc_weights[0], acc_weights[1], acc_weights[2], acc_weights[3],...]
    psum x0 -> x1, waiting for transfers between devices: none -> 32.3 us  [local(): summed = lax.psum(inner, 'tower')]
    reduce_scatter x1, waiting for transfers between devices: 0.01 us -> 24.4 us  [local(): lax.psum_scatter(acc_dh, 'plate', scatter_dimension=0, tiled=True)]
  transfers between devices with their start and end apart: 8 -> 9, of which waited for: 1 -> 5; matrix products, arithmetic and copies ran while one was open for 0% -> 0% of each run, Pallas kernels for 0% -> 0%
where the time goes in v1:
time: 1120 us; the launch traced here: 1110 us
  waiting for transfers between devices  728 us (65%)
  loops' own time  202 us (18%)
  blocking collectives  43.3 us (4%)
  matrix products  39.8 us (4%)
  other arithmetic  37.1 us (3%)
  local copies, waits for them, and re-layouts  34.4 us (3%)
  between operations  16 us (1%)
    psum x1, waiting for transfers between devices, local(): lax.psum((acc_weights[0], acc_weights[1], acc_weights[2], acc_weights[3],...  669 us
    another operation x1, loops' own time, local(): lax.fori_loop(0, tile_counts[0, 0], visit_listed, initial)  202 us
    psum x1, waiting for transfers between devices, local(): summed = lax.psum(inner, 'tower')  32.3 us
    reduce_scatter x1, waiting for transfers between devices, local(): lax.psum_scatter(acc_dh, 'plate', scatter_dimension=0, tiled=True)  24.4 us
  transfers between devices with their start and end apart: 9, of which 5 were waited for; matrix products, arithmetic and copies ran while one was open for 0% of the time, Pallas kernels for 0%

profile of v1, /device:TPU:1, one launch (start us, length us, event | category | flops | bytes accessed | tf_op | source)
XLA Modules:
  0.0 1111.9 jit_solution(10729105198202971981)
XLA Ops:
  7.9 1.0 bitcast_select_fusion
  8.9 2.1 collective-permute-start.2
  10.9 3.1 collective-permute-start.3
  14.1 4.2 collective-permute-start.1
  18.2 6.5 all-gather
  24.7 5.9 all_gather.7
  30.9 0.6 copy-done.6
  31.5 304.3 %while.25 = (s32[]{:T(128)}, f32[4,256,128]{2,1,0:T(8,128)S(1)}, f32[4,3,256]{2,1,0:T(4,128)S(1)}, f32[3,768]{1,0:T(4,128)S(1)}, f32[16,128]{1,0:T(8,128)S(1)}, ...) while((s32[]{:T(128)}, f32[4,256,128]{2,1,0:T(8,128)S(1)}, ...), condition=%wide.region_8.9_spmd, body=%wide.region_0.8_spmd.sunk | while | flops 118017312 | bytes 6281055 | solution.py:171
  35.4 0.6 fusion.71
  42.9 0.6 fusion.73
  52.3 0.6 fusion.71
  57.5 0.6 constant_dynamic-slice_fusion.10
  59.8 0.6 fusion.73
  69.1 0.6 fusion.71
  74.4 0.6 constant_dynamic-slice_fusion.10
  76.6 0.6 fusion.73
  86.1 0.6 fusion.71
  91.3 0.6 constant_dynamic-slice_fusion.10
  93.5 0.6 fusion.73
  103.0 0.6 fusion.71
  108.2 0.6 constant_dynamic-slice_fusion.10
  110.5 0.6 fusion.73
  119.8 0.6 fusion.71
  127.3 0.6 fusion.73
  136.7 0.6 fusion.71
  142.0 0.6 constant_dynamic-slice_fusion.10
  144.2 0.6 fusion.73
  153.6 0.6 fusion.71
  161.1 0.6 fusion.73
  170.5 0.6 fusion.71
  175.7 0.6 constant_dynamic-slice_fusion.10
  177.9 0.6 fusion.73
  187.4 0.6 fusion.71
  192.6 0.6 constant_dynamic-slice_fusion.10
  194.8 0.6 fusion.73
  204.3 0.6 fusion.71
  211.8 0.6 fusion.73
  221.2 0.6 fusion.71
  228.7 0.6 fusion.73
  238.0 0.6 fusion.71
  245.5 0.6 fusion.73
  254.7 0.6 fusion.71
  262.2 0.6 fusion.73
  271.6 0.6 fusion.71
  279.0 0.6 fusion.73
  288.5 0.6 fusion.71
  296.0 0.6 fusion.73
  305.3 0.6 fusion.71
  312.8 0.6 fusion.73
  322.1 0.6 fusion.71
  329.6 0.6 fusion.73
  335.9 0.6 copy-done.1
  336.6 668.9 %all-reduce.6.cloned.1.call-done = f32[128,128]{1,0:T(8,128)} async-done(((f32[128,128]{1,0:T(8,128)}), f32[128,128]{1,0:T(8,128)}) %all-reduce.6.cloned.1.call-update) | async-done | bytes 65552 | tf_op jit(solution)/shard_map/psum | solution.py:184
  1006.2 0.6 copy-done.10
  1007.4 12.5 %all-reduce.2 = (f32[4,3,256]{2,1,0:T(4,128)S(1)}, f32[16,128]{1,0:T(8,128)S(1)}, f32[]{:T(128)}, f32[128]{0:T(128)S(1)}, f32[128]{0:T(128)S(1)}) all-reduce(f32[4,3,256]{2,1,0:T(4,128)S(1)} %get-tuple-element.333, f32[16,128]{1,0:T(8,128)S(1)} %get-tuple-element.335, ...), channel_id=4, replica_groups=mesh['tower'=8,'plate'=4] {'plate'}, use_global_device_ids=true, to_apply=%region_10.11.clone | all-reduce | flops 5377 | bytes 43016
  1019.9 18.4 %all-reduce.1 = (f32[16,128]{1,0:T(8,128)S(1)}, f32[]{:T(128)}, f32[128]{0:T(128)S(1)}, f32[128]{0:T(128)S(1)}) all-reduce(f32[16,128]{1,0:T(8,128)S(1)} %get-tuple-element.398, f32[]{:T(128)} %get-tuple-element.399, f32[128]{0:T(128)S(1)} %get-tuple-element.400, ...), channel_id=1, replica_groups=mesh['tower'=8,'plate'=4] {'tower'}, use_global_device_ids=true, to_apply=%region_12.13 | all-reduce | flops 2305 | bytes 18440 | tf_op jit(solution)/shard_map/psum | solution.py:187
  1039.1 1.5 collective-permute-start.5
  1040.6 0.6 broadcast_multiply_fusion.3
  1041.9 2.5 collective-permute-done.5
  1044.4 0.7 fusion.28
  1045.6 32.3 %all-reduce.8.cloned.1.call-done = f32[128,128]{1,0:T(8,128)} async-done(((f32[128,128]{1,0:T(8,128)}), f32[128,128]{1,0:T(8,128)}) %all-reduce.8.cloned.1.call-update) | async-done | bytes 65552 | tf_op jit(solution)/shard_map/psum | solution.py:187
  1077.9 1.5 broadcast_multiply_fusion.2
  1079.3 24.4 %reduce-scatter.2.cloned.1.call-done = f32[1,256,128]{2,1,0:T(8,128)} async-done(((f32[4,256,128]{2,1,0:T(8,128)}), f32[1,256,128]{2,1,0:T(8,128)}) %reduce-scatter.2.cloned.1.call-update) | async-done | bytes 131088 | tf_op jit(solution)/shard_map/reduce_scatter | solution.py:175
  1103.7 1.7 broadcast_select_fusion
  (544 shorter events, 78.7 us)
Async XLA Ops:
  7.2 998.3 %all-reduce.6.cloned.1.call-start = ((), (), s32[]{:S(2)}) async-start(), calls=%async_computation.2 | async-start | bytes 131072 | tf_op jit(solution)/shard_map/psum | solution.py:184
  8.8 5.2 copy-start.5
  8.9 21.8 %collective-permute-start.2 = (bf16[256,128]{1,0:T(8,128)(2,1)S(1)}, bf16[256,128]{1,0:T(8,128)(2,1)S(1)}, u32[]{:S(2)}, u32[]{:S(2)}) collective-permute-start(bf16[256,128]{1,0:T(8,128)(2,1)S(1)} %get-tuple-element.421), channel_id=1, source_target_pairs={{28,0},{0,4},{4,8},{8,12},{12,16},{16,20},{20,24},{24,28},{29,1},{... | collective-permute-start | bytes 196616 | tf_op jit(solution)/shard_map/ppermute | solution.py:19
  10.9 19.7 %collective-permute-start.3 = (bf16[256,128]{1,0:T(8,128)(2,1)S(1)}, bf16[256,128]{1,0:T(8,128)(2,1)S(1)}, u32[]{:S(2)}, u32[]{:S(2)}) collective-permute-start(bf16[256,128]{1,0:T(8,128)(2,1)S(1)} %get-tuple-element.421), channel_id=1, source_target_pairs={{4,0},{8,4},{12,8},{16,12},{20,16},{24,20},{28,24},{0,28},{5,1},{9... | collective-permute-start | bytes 196616 | tf_op jit(solution)/shard_map/ppermute | solution.py:19
  14.1 16.6 %collective-permute-start = (bf16[3,256]{1,0:T(4,128)(2,1)S(1)}, bf16[3,256]{1,0:T(4,128)(2,1)S(1)}, u32[]{:S(2)}, u32[]{:S(2)}) collective-permute-start(bf16[3,256]{1,0:T(4,128)(2,1)S(1)} %bitcast.114), channel_id=1, source_target_pairs={{28,0},{0,4},{4,8},{8,12},{12,16},{16,20},{20,24},{24,28},{29,1},{... | collective-permute-start | bytes 4616 | tf_op jit(solution)/shard_map/ppermute | solution.py:19
  14.1 16.6 %collective-permute-start.1 = (bf16[3,256]{1,0:T(4,128)(2,1)S(1)}, bf16[3,256]{1,0:T(4,128)(2,1)S(1)}, u32[]{:S(2)}, u32[]{:S(2)}) collective-permute-start(bf16[3,256]{1,0:T(4,128)(2,1)S(1)} %bitcast.115), channel_id=1, source_target_pairs={{4,0},{8,4},{12,8},{16,12},{20,16},{24,20},{28,24},{0,28},{5,1},{9... | collective-permute-start | bytes 4616 | tf_op jit(solution)/shard_map/ppermute | solution.py:19
  30.8 0.8 copy-start.6
  30.8 0.7 copy-start.8
  30.8 0.7 copy-start.9
  30.8 0.7 copy-start.2
  30.8 0.7 copy-start.3
  30.9 0.7 copy-start.4
  30.9 0.7 copy-start.7
  335.9 0.6 copy-start.1
  335.9 703.2 %copy-start = (f32[4,256,128]{2,1,0:T(8,128)}, f32[4,256,128]{2,1,0:T(8,128)S(1)}, u32[]{:S(2)}) copy-start(f32[4,256,128]{2,1,0:T(8,128)S(1)} %get-tuple-element.332) | copy-start | bytes 1572868
  336.5 741.4 %all-reduce.8.cloned.1.call-start = ((), (), s32[]{:S(2)}) async-start(), calls=%async_computation.3 | async-start | bytes 131072 | tf_op jit(solution)/shard_map/psum | solution.py:187
  1005.5 98.2 %reduce-scatter.2.cloned.1.call-start = ((), (), s32[]{:S(2)}) async-start(), calls=%async_computation.1 | async-start | bytes 655360 | tf_op jit(solution)/shard_map/reduce_scatter | solution.py:175
  1006.2 0.7 copy-start.10
  1039.1 2.8 collective-permute-start.4
  1039.1 5.2 collective-permute-start.5
Sparse Core Ops, SparseCore 0:
  336.6 668.7 all-reduce.5
  1008.9 68.9 all-reduce.7
  1080.4 23.2 reduce-scatter.1
